TPU v7x, 32 devices: a whole 2x2x4 slice. The times are simulated.
32 devices in a mesh: parts: 2 (over x), wide: 16 (over z, y, core).
Axes of the slice: x: 2, y: 2, z: 4, core: 2. Of those that a mesh axis runs over, the one named last changes fastest.
Arguments:
- voxels: bfloat16 [32768, 256], P(('parts', 'wide')), parts along dimension 0, may hold values from -16 to 16
- regular_window: int32 [32768], P(('parts', 'wide')), parts along dimension 0, may hold values from 0 to 127, never falling along the last dimension, each value on 1 to 256 neighbouring positions
- shifted_window: int32 [32768], P(('parts', 'wide')), parts along dimension 0, may hold values from 0 to 127, never falling along the last dimension, each value on 1 to 256 neighbouring positions
- dest: int32 [32768], P(('parts', 'wide')), parts along dimension 0, may hold values from 0 to 16383, as said below
- w_qkv: bfloat16 [2, 256, 768], replicated, may hold values from -0.375 to 0.375
- w_out: bfloat16 [2, 256, 256], replicated, may hold values from -1.5 to 1.5
- gain: float32 [2, 256], replicated, may hold values from 0.1 to 1.9
- temper: float32 [2, 8], replicated, may hold values from 0.5 to 6
Outputs:
- shifted_out: bfloat16 [32768, 256], P(('parts', 'wide')), parts along dimension 0
There are 2 independent parts, one for each index of `parts`. A program takes and returns all parts, laid end to end along the dimension named above; an argument that names none is the same for every part. Nothing has to cross between parts.
Inputs may be any that keep to these rules, and one draw needn't show every extreme that they name: `regular_window`: window ids never fall along the order; every window has 1 to 256 voxels and one has exactly 256. `shifted_window`: window ids never fall along the order; every window has 1 to 256 voxels and one has exactly 256. dest is a permutation. Counting blocks of 1024 consecutive positions, at most 128 voxels go from one block of the regular order to one block of the shifted order, and some pair reaches 128; the count from a block to the block k places further along, cyclically, is the same for every block.
All inputs are finite; a program needn't handle non-finite values.
Results may differ from a plain program's by a relative error of at most 0.007.
The roundings to bfloat16 on the way count: a program that leaves them out, or rounds other values in their place, can miss the bound.
Values may be sent and summed in bfloat16 or wider, within the bound.
A program may use at most 64 MiB of HBM per device.

v0:
```python
import functools
import math

import jax
import jax.numpy as jnp
from jax import lax
from jax.experimental import pallas as pl
from jax.experimental.pallas import tpu as pltpu
from jax.sharding import PartitionSpec as P

HEADS = 8
LANES = 128
GROUPS = 2

epsilon = 1e-05
apart = 2.0**100

BF = jnp.bfloat16
F32 = jnp.float32
NT = (((1,), (1,)), ((), ()))


def bit_flags(marks_row):
    count = marks_row.shape[1]
    place = lax.broadcasted_iota(jnp.int32, (LANES, count), 0)
    bit = (jnp.broadcast_to(marks_row, (LANES, count)) >> (place & 31)) & 1
    return jnp.where(place < LANES // 2, bit, 1 - bit).astype(F32)


def project_keys(h, marks_row, w, k_ref, v_ref, first):
    rows, channels = h.shape
    half = channels // GROUPS
    kv = jnp.dot(h, w[:, channels:], preferred_element_type=F32)
    code = ((bit_flags(marks_row) - 1.0) * apart).astype(BF)
    at = pl.ds(first, rows)
    for g in range(GROUPS):
        k_ref[g, :half, at] = jnp.transpose(kv[:, g * half : (g + 1) * half]).astype(BF)
        k_ref[g, half:, at] = code
        v_ref[g, at, :] = kv[:, channels + g * half : channels + (g + 1) * half].astype(BF)


def attend(h, marks_row, layer, fac_ref, w, w_out, gain_row, k_ref, v_ref, q_ref, a_ref, first_key, key_rows):
    rows, channels = h.shape
    half = channels // GROUPS
    head_dim = channels // HEADS
    each = HEADS // GROUPS
    q = jnp.dot(h, w[:, :channels], preferred_element_type=F32).astype(BF)
    code = jnp.transpose(bit_flags(marks_row)).astype(BF)
    head_of_lane = lax.broadcasted_iota(jnp.int32, (rows, half), 1) // head_dim
    for g in range(GROUPS):
        q_ref[g] = q[:, g * half : (g + 1) * half]

    def group(g, carry):
        q_half = q_ref[g]
        keys = k_ref[g, :, pl.ds(first_key, key_rows)]
        values = v_ref[g, pl.ds(first_key, key_rows), :]
        out = jnp.zeros((rows, half), F32)
        for j in range(each):
            mine = head_of_lane == j
            query = jnp.concatenate([jnp.where(mine, q_half, jnp.zeros_like(q_half)), code], axis=1)
            s = jnp.dot(query, keys, preferred_element_type=F32)
            top = jnp.max(s, axis=1, keepdims=True)
            e = jnp.exp2((s - top) * fac_ref[layer, g * each + j])
            p = (e * (1.0 / jnp.sum(e, axis=1, keepdims=True))).astype(BF)
            out = jnp.where(mine, jnp.dot(p, values, preferred_element_type=F32), out)
        a_ref[g] = out.astype(BF)
        return carry

    lax.fori_loop(0, GROUPS, group, 0)
    attended = jnp.concatenate([a_ref[g] for g in range(GROUPS)], axis=1)
    summed = h.astype(F32) + jnp.dot(attended, w_out, preferred_element_type=F32)
    center = jnp.mean(summed, axis=1, keepdims=True)
    shifted = summed - center
    spread = jnp.mean(jnp.square(shifted), axis=1, keepdims=True)
    return (shifted * lax.rsqrt(spread + epsilon) * gain_row).astype(BF)


def whole_kernel(
    n, fac_ref, h_ref, marks_ref, dest_ref, w_ref, wo_ref, gain_ref, out_ref,
    k_ref, v_ref, q_ref, a_ref, first_ref, moved_ref, low_ref, high_ref, mlow_ref, mhigh_ref,
    outgoing, arrived, slots_out, slots_in, halo_send, halo_recv, slot_send, slot_recv, row_send, row_recv,
):
    rows, channels = h_ref.shape
    rim = rows // 4
    block = rim
    capacity = outgoing.shape[1]
    me = lax.axis_index("wide")
    right, left = lax.rem(me + 1, n), lax.rem(me + n - 1, n)

    barrier = pltpu.get_barrier_semaphore()

    def greet(t, carry):
        pl.semaphore_signal(
            barrier, inc=1, device_id={"wide": lax.rem(me + t, n)}, device_id_type=pl.DeviceIdType.MESH
        )
        return carry

    lax.fori_loop(1, n, greet, 0)

    def remote(src, dst, send, recv, peer):
        return pltpu.make_async_remote_copy(
            src_ref=src, dst_ref=dst, send_sem=send, recv_sem=recv,
            device_id={"wide": peer}, device_id_type=pl.DeviceIdType.MESH,
        )

    dest = dest_ref[...]
    target = lax.div(dest, jnp.full_like(dest, rows))
    slot = dest - target * rows + 1
    member = lax.broadcasted_iota(jnp.int32, (n, rows), 0) == jnp.broadcast_to(target, (n, rows))
    member = member.astype(F32)
    upper = (
        lax.broadcasted_iota(jnp.int32, (block, block), 0) <= lax.broadcasted_iota(jnp.int32, (block, block), 1)
    ).astype(F32).astype(BF)
    carry = jnp.zeros((n, 1), F32)
    ranks = []
    for r in range(0, rows, block):
        part = member[:, r : r + block]
        ranks.append(jnp.dot(part.astype(BF), upper, preferred_element_type=F32) + carry)
        carry = carry + jnp.sum(part, axis=1, keepdims=True)
    rank = jnp.sum(jnp.concatenate(ranks, axis=1) * member, axis=0, keepdims=True)
    position = rank.astype(jnp.int32) - 1
    width = slots_out.shape[2]
    chosen = (
        lax.broadcasted_iota(jnp.int32, (width, rows), 0) == jnp.broadcast_to(position, (width, rows))
    ).astype(F32).astype(BF)
    coarse = (member * (slot >> 5).astype(F32)).astype(BF)
    fine = (member * (slot & 31).astype(F32)).astype(BF)
    table = lax.dot_general(coarse, chosen, NT, preferred_element_type=F32) * 32.0
    table = (table + lax.dot_general(fine, chosen, NT, preferred_element_type=F32)).astype(jnp.int32)
    for t in range(n):
        slots_out[t] = table[t : t + 1, :]

    for r in range(0, rows, block):
        project_keys(h_ref[r : r + block, :], marks_ref[0:1, r : r + block], w_ref[0], k_ref, v_ref, rim + r)

    pl.semaphore_wait(barrier, n - 1)

    early = (
        (h_ref.at[pl.ds(0, rim)], high_ref.at[0], 0, left),
        (h_ref.at[pl.ds(rows - rim, rim)], low_ref.at[0], 1, right),
        (marks_ref.at[:, pl.ds(0, rim)], mhigh_ref, 2, left),
        (marks_ref.at[:, pl.ds(rows - rim, rim)], mlow_ref, 3, right),
    )
    late = (
        (moved_ref.at[pl.ds(0, rim)], high_ref.at[1], 4, left),
        (moved_ref.at[pl.ds(rows - rim, rim)], low_ref.at[1], 5, right),
    )

    def rim_copy(entry):
        src, dst, number, peer = entry
        return remote(src, dst, halo_send.at[number], halo_recv.at[number], peer)

    for entry in early:
        rim_copy(entry).start()

    def slot_copy(peer, source):
        return remote(slots_out.at[peer], slots_in.at[source], slot_send.at[peer], slot_recv.at[source], peer)

    def send_slots(t, carry):
        slot_copy(lax.rem(me + t, n), me).start()
        return carry

    lax.fori_loop(1, n, send_slots, 0)
    slots_in[me] = slots_out[me]

    def layer_blocks(layer, h_of, store, step, start):
        def one(i, carry):
            r = pl.multiple_of(block * (start + step * i), block)
            store[pl.ds(r, block), :] = attend(
                h_of[pl.ds(r, block), :],
                marks_ref[layer : layer + 1, pl.ds(r, block)],
                layer, fac_ref, w_ref[layer], wo_ref[layer], gain_ref[layer : layer + 1, :],
                k_ref, v_ref, q_ref, a_ref, r, block + 2 * rim,
            )
            return carry

        lax.fori_loop(0, 2, one, 0)

    def layer_rims(layer):
        project_keys(low_ref[layer], mlow_ref[layer : layer + 1, :], w_ref[layer], k_ref, v_ref, 0)
        project_keys(high_ref[layer], mhigh_ref[layer : layer + 1, :], w_ref[layer], k_ref, v_ref, rim + rows)

    layer_blocks(0, h_ref, first_ref, 1, 1)
    for entry in early:
        rim_copy(entry).wait()
    layer_rims(0)
    layer_blocks(0, h_ref, first_ref, 3, 0)

    first = first_ref[...]
    place = lax.broadcasted_iota(jnp.int32, (capacity, rows), 0)

    def gathered(peer):
        wanted = jnp.where(target == peer, position, -1)
        pick = (place == jnp.broadcast_to(wanted, (capacity, rows))).astype(F32).astype(BF)
        return jnp.dot(pick, first, preferred_element_type=F32).astype(BF)

    def peer_at(t):
        odd = lax.rem(t, 2)
        return lax.rem(me + n // 2 + (2 * odd - 1) * ((t + 1) // 2) + n, n)

    def row_copy(peer, source):
        return remote(outgoing.at[peer], arrived.at[source], row_send.at[peer], row_recv.at[source], peer)

    outgoing[peer_at(0)] = gathered(peer_at(0))

    def exchange(t, carry):
        peer = peer_at(t)
        outgoing[peer] = gathered(peer)
        row_copy(peer_at(t - 1), me).start()
        return carry

    lax.fori_loop(1, n - 1, exchange, 0)
    arrived[me] = gathered(me)
    row_copy(peer_at(n - 2), me).start()

    def settle_copies(t, carry):
        other = lax.rem(me + t, n)
        slot_copy(other, other).wait()
        row_copy(other, other).wait()
        return carry

    lax.fori_loop(1, n, settle_copies, 0)

    places = jnp.concatenate([slots_in[t][:, :capacity] for t in range(n)], axis=1)
    came = arrived[...].reshape(n * capacity, channels)

    def land(r):
        here = lax.broadcasted_iota(jnp.int32, (block, n * capacity), 0) + (r + 1)
        pick = (here == jnp.broadcast_to(places, (block, n * capacity))).astype(F32).astype(BF)
        moved_ref[r : r + block, :] = jnp.dot(pick, came, preferred_element_type=F32).astype(BF)

    def own_keys(r):
        project_keys(moved_ref[r : r + block, :], marks_ref[1:2, r : r + block], w_ref[1], k_ref, v_ref, rim + r)

    land(0)
    land(rows - block)
    land(block)
    for entry in late:
        rim_copy(entry).start()
    land(2 * block)
    for r in range(0, rows, block):
        own_keys(r)
    layer_blocks(1, moved_ref, out_ref, 1, 1)
    for entry in late:
        rim_copy(entry).wait()
    layer_rims(1)
    layer_blocks(1, moved_ref, out_ref, 3, 0)


def body(voxels, regular_window, shifted_window, dest, w_qkv, w_out, gain, temper):
    rows, channels = voxels.shape
    n = lax.axis_size("wide")
    rim = rows // 4
    half = channels // GROUPS
    capacity = 2 * rows // n
    factor = temper * (1.0 / math.sqrt(channels // HEADS)) * math.log2(math.e)
    marks = jnp.stack([regular_window, shifted_window]) + 1
    vmem = pl.BlockSpec(memory_space=pltpu.VMEM)
    dma = pltpu.SemaphoreType.DMA
    return pl.pallas_call(
        functools.partial(whole_kernel, n),
        out_shape=jax.ShapeDtypeStruct((rows, channels), BF),
        in_specs=[pl.BlockSpec(memory_space=pltpu.SMEM)] + [vmem] * 6,
        out_specs=vmem,
        scratch_shapes=[
            pltpu.VMEM((GROUPS, half + LANES, rows + 2 * rim), BF),
            pltpu.VMEM((GROUPS, rows + 2 * rim, half), BF),
            pltpu.VMEM((GROUPS, rim, half), BF),
            pltpu.VMEM((GROUPS, rim, half), BF),
            pltpu.VMEM((rows, channels), BF),
            pltpu.VMEM((rows, channels), BF),
            pltpu.VMEM((2, rim, channels), BF),
            pltpu.VMEM((2, rim, channels), BF),
            pltpu.VMEM((2, rim), jnp.int32),
            pltpu.VMEM((2, rim), jnp.int32),
            pltpu.VMEM((n, capacity, channels), BF),
            pltpu.VMEM((n, capacity, channels), BF),
            pltpu.VMEM((n, 1, max(capacity, LANES)), jnp.int32),
            pltpu.VMEM((n, 1, max(capacity, LANES)), jnp.int32),
            dma((6,)), dma((6,)), dma((n,)), dma((n,)), dma((n,)), dma((n,)),
        ],
        compiler_params=pltpu.CompilerParams(
            vmem_limit_bytes=48 << 20, collective_id=0, has_side_effects=True
        ),
    )(factor, voxels, marks, dest[None, :], w_qkv, w_out, gain)


def solution(mesh):
    spread = P(("parts", "wide"))
    wide_rows = P(("parts", "wide"), None)
    return jax.shard_map(
        body,
        mesh=mesh,
        in_specs=(wide_rows, spread, spread, spread, P(), P(), P(), P()),
        out_specs=wide_rows,
        check_vma=False,
    )
```

profile of v0, /device:TPU:13, one launch (start us, length us, event | category | flops | bytes accessed | tf_op | source)
XLA Modules:
  0.0 78.7 jit_solution(6800366864620954084)
XLA Ops:
  0.0 0.0 copy-start.5
  0.0 0.0 copy-start.6
  0.0 0.7 copy-done.6
  0.7 0.0 copy-done.5
  0.7 0.0 copy-start.3
  0.7 0.0 copy-start.4
  0.7 0.7 add_add_fusion.marks_ref
  1.4 0.0 copy-done.3
  1.4 0.0 copy-done.4
  1.5 0.0 copy-start
  1.5 1.1 %copy-done = bf16[2,256,768]{2,1,0:T(8,128)(2,1)S(1)} copy-done((bf16[2,256,768]{2,1,0:T(8,128)(2,1)S(1)}, bf16[2,256,768]{2,1,0:T(8,128)(2,1)}, u32[]{:S(2)}) %copy-start) | copy-done | bytes 786456
  2.6 0.0 copy-start.1
  2.6 1.0 %copy-done.1 = bf16[1024,256]{1,0:T(8,128)(2,1)S(1)} copy-done((bf16[1024,256]{1,0:T(8,128)(2,1)S(1)}, bf16[1024,256]{1,0:T(8,128)(2,1)}, u32[]{:S(2)}) %copy-start.1) | copy-done | bytes 524312
  3.6 0.0 copy-start.2
  3.6 0.9 %copy-done.2 = bf16[2,256,256]{2,1,0:T(8,128)(2,1)S(1)} copy-done((bf16[2,256,256]{2,1,0:T(8,128)(2,1)S(1)}, bf16[2,256,256]{2,1,0:T(8,128)(2,1)}, u32[]{:S(2)}) %copy-start.2) | copy-done | bytes 262168
  4.6 73.3 %shard_map.82 = bf16[1024,256]{1,0:T(8,128)(2,1)S(1)} custom-call(f32[2,8]{1,0:T(2,128)S(1)} %broadcast_multiply_fusion.fac_ref, bf16[1024,256]{1,0:T(8,128)(2,1)S(1)} %copy-done.1, s32[2,1024]{1,0:T(2,128)S(1)} %add_add_fusion.marks_ref, s32[1,1024]{1,0:T(1,128)S(1)} %bitcast.3, bf16[2,256,768]{2,1,0:T(8,128)(2,1)S(1)} %copy-done, ...), custom_call_target="tpu_custom_call" | custom-call | tf_op jit(solution)/shard_map/pallas_call | solution.py:260
  77.9 0.8 %copy.10 = bf16[1024,256]{1,0:T(8,128)(2,1)} copy(bf16[1024,256]{1,0:T(8,128)(2,1)S(1)} %shard_map.82) | data formatting | bytes 1048576
  (1 shorter events, 0.0 us)
Async XLA Ops:
  0.0 0.7 copy-start.5
  0.0 0.7 copy-start.6
  0.7 0.7 copy-start.3
  0.7 0.7 copy-start.4
  1.5 1.1 %copy-start = (bf16[2,256,768]{2,1,0:T(8,128)(2,1)S(1)}, bf16[2,256,768]{2,1,0:T(8,128)(2,1)}, u32[]{:S(2)}) copy-start(bf16[2,256,768]{2,1,0:T(8,128)(2,1)} %w_ref.1) | copy-start | bytes 2359300
  2.6 1.0 %copy-start.1 = (bf16[1024,256]{1,0:T(8,128)(2,1)S(1)}, bf16[1024,256]{1,0:T(8,128)(2,1)}, u32[]{:S(2)}) copy-start(bf16[1024,256]{1,0:T(8,128)(2,1)} %h_ref.1) | copy-start | bytes 1572868
  3.6 0.9 %copy-start.2 = (bf16[2,256,256]{2,1,0:T(8,128)(2,1)S(1)}, bf16[2,256,256]{2,1,0:T(8,128)(2,1)}, u32[]{:S(2)}) copy-start(bf16[2,256,256]{2,1,0:T(8,128)(2,1)} %wo_ref.1) | copy-start | bytes 786436
where the time goes:
time: 79.6 us; the launch traced here: 78.7 us
  Pallas kernels  73.3 us (92%)
  local copies, waits for them, and re-layouts  4.62 us (6%)
    pallas_call x1, Pallas kernels, body(): pl.pallas_call(functools.partial(whole_kernel, n), out_shape=jax.ShapeDty...  73.3 us
    unnamed x15, local copies, waits for them, and re-layouts  4.62 us

commit v1 on v0

--- a/solution.py
+++ b/solution.py
@@ -39,7 +39,7 @@
         v_ref[g, at, :] = kv[:, channels + g * half : channels + (g + 1) * half].astype(BF)
 
 
-def attend(h, marks_row, layer, fac_ref, w, w_out, gain_row, k_ref, v_ref, q_ref, a_ref, first_key, key_rows):
+def attend(h, marks_row, layer, fac_ref, w, w_out, gain_row, k_ref, v_ref, first_key, key_rows):
     rows, channels = h.shape
     half = channels // GROUPS
     head_dim = channels // HEADS
@@ -47,27 +47,40 @@
     q = jnp.dot(h, w[:, :channels], preferred_element_type=F32).astype(BF)
     code = jnp.transpose(bit_flags(marks_row)).astype(BF)
     head_of_lane = lax.broadcasted_iota(jnp.int32, (rows, half), 1) // head_dim
-    for g in range(GROUPS):
-        q_ref[g] = q[:, g * half : (g + 1) * half]
-
-    def group(g, carry):
-        q_half = q_ref[g]
-        keys = k_ref[g, :, pl.ds(first_key, key_rows)]
-        values = v_ref[g, pl.ds(first_key, key_rows), :]
-        out = jnp.zeros((rows, half), F32)
-        for j in range(each):
-            mine = head_of_lane == j
-            query = jnp.concatenate([jnp.where(mine, q_half, jnp.zeros_like(q_half)), code], axis=1)
-            s = jnp.dot(query, keys, preferred_element_type=F32)
+    pairs = [(g, j) for g in range(GROUPS) for j in range(0, each, 2)]
+
+    def scores(pair):
+        g, first = pair
+        q_half = q[:, g * half : (g + 1) * half]
+        stacked = jnp.concatenate(
+            [
+                jnp.concatenate([jnp.where(head_of_lane == j, q_half, jnp.zeros_like(q_half)), code], axis=1)
+                for j in (first, first + 1)
+            ],
+            axis=0,
+        )
+        return jnp.dot(stacked, k_ref[g, :, pl.ds(first_key, key_rows)], preferred_element_type=F32)
+
+    outs = [jnp.zeros((rows, half), F32) for _ in range(GROUPS)]
+    coming = scores(pairs[0])
+    for t, (g, first) in enumerate(pairs):
+        both = coming
+        if t + 1 < len(pairs):
+            coming = scores(pairs[t + 1])
+        weights = []
+        for i in range(2):
+            s = both[i * rows : (i + 1) * rows]
             top = jnp.max(s, axis=1, keepdims=True)
-            e = jnp.exp2((s - top) * fac_ref[layer, g * each + j])
-            p = (e * (1.0 / jnp.sum(e, axis=1, keepdims=True))).astype(BF)
-            out = jnp.where(mine, jnp.dot(p, values, preferred_element_type=F32), out)
-        a_ref[g] = out.astype(BF)
-        return carry
-
-    lax.fori_loop(0, GROUPS, group, 0)
-    attended = jnp.concatenate([a_ref[g] for g in range(GROUPS)], axis=1)
+            e = jnp.exp2((s - top) * fac_ref[layer, g * each + first + i])
+            weights.append((e * (1.0 / jnp.sum(e, axis=1, keepdims=True))).astype(BF))
+        o = jnp.dot(
+            jnp.concatenate(weights, axis=0),
+            v_ref[g, pl.ds(first_key, key_rows), :],
+            preferred_element_type=F32,
+        )
+        for i in range(2):
+            outs[g] = jnp.where(head_of_lane == first + i, o[i * rows : (i + 1) * rows], outs[g])
+    attended = jnp.concatenate([o.astype(BF) for o in outs], axis=1)
     summed = h.astype(F32) + jnp.dot(attended, w_out, preferred_element_type=F32)
     center = jnp.mean(summed, axis=1, keepdims=True)
     shifted = summed - center
@@ -77,7 +90,7 @@
 
 def whole_kernel(
     n, fac_ref, h_ref, marks_ref, dest_ref, w_ref, wo_ref, gain_ref, out_ref,
-    k_ref, v_ref, q_ref, a_ref, first_ref, moved_ref, low_ref, high_ref, mlow_ref, mhigh_ref,
+    k_ref, v_ref, first_ref, moved_ref, low_ref, high_ref, mlow_ref, mhigh_ref,
     outgoing, arrived, slots_out, slots_in, halo_send, halo_recv, slot_send, slot_recv, row_send, row_recv,
 ):
     rows, channels = h_ref.shape
@@ -170,7 +183,7 @@
                 h_of[pl.ds(r, block), :],
                 marks_ref[layer : layer + 1, pl.ds(r, block)],
                 layer, fac_ref, w_ref[layer], wo_ref[layer], gain_ref[layer : layer + 1, :],
-                k_ref, v_ref, q_ref, a_ref, r, block + 2 * rim,
+                k_ref, v_ref, r, block + 2 * rim,
             )
             return carry
 
@@ -265,8 +278,6 @@
         scratch_shapes=[
             pltpu.VMEM((GROUPS, half + LANES, rows + 2 * rim), BF),
             pltpu.VMEM((GROUPS, rows + 2 * rim, half), BF),
-            pltpu.VMEM((GROUPS, rim, half), BF),
-            pltpu.VMEM((GROUPS, rim, half), BF),
             pltpu.VMEM((rows, channels), BF),
             pltpu.VMEM((rows, channels), BF),
             pltpu.VMEM((2, rim, channels), BF),

time: 79.6 us -> 61.4 us (0.77)
  Pallas kernels: 73.3 us -> 55.3 us
    pallas_call x1, Pallas kernels: 73.3 us -> 55.3 us  [body(): pl.pallas_call(functools.partial(whole_kernel, n), out_shape=jax.ShapeDty...]
where the time goes in v1:
time: 61.4 us; the launch traced here: 60.6 us
  Pallas kernels  55.3 us (90%)
  local copies, waits for them, and re-layouts  4.62 us (8%)
  other arithmetic  0.72 us (1%)
    pallas_call x1, Pallas kernels, body(): pl.pallas_call(functools.partial(whole_kernel, n), out_shape=jax.ShapeDty...  55.3 us
    unnamed x15, local copies, waits for them, and re-layouts  4.62 us

profile of v1, /device:TPU:13, one launch (start us, length us, event | category | flops | bytes accessed | tf_op | source)
XLA Modules:
  0.0 60.6 jit_solution(12396850672506184343)
XLA Ops:
  0.0 0.0 copy-start.5
  0.0 0.0 copy-start.6
  0.0 0.7 %copy-done.6 = f32[2,8]{1,0:T(2,128)S(1)} copy-done((f32[2,8]{1,0:T(2,128)S(1)}, f32[2,8]{1,0:T(2,128)}, u32[]{:S(2)}) %copy-start.6) | copy-done | bytes 88
  0.7 0.0 copy-done.5
  0.7 0.0 copy-start.3
  0.7 0.0 copy-start.4
  0.7 0.7 %add_add_fusion.marks_ref = s32[2,1024]{1,0:T(2,128)S(1)} fusion(s32[1,1024]{1,0:T(1,128)S(1)} %bitcast.4, s32[1,1024]{1,0:T(1,128)} %bitcast.5), kind=kLoop, calls=%fused_computation | loop fusion | flops 4096 | bytes 16384 | tf_op jit(solution)/shard_map/add | solution.py:270
  1.4 0.0 copy-done.3
  1.4 0.0 copy-done.4
  1.5 0.0 copy-start
  1.5 1.1 %copy-done = bf16[2,256,768]{2,1,0:T(8,128)(2,1)S(1)} copy-done((bf16[2,256,768]{2,1,0:T(8,128)(2,1)S(1)}, bf16[2,256,768]{2,1,0:T(8,128)(2,1)}, u32[]{:S(2)}) %copy-start) | copy-done | bytes 786456
  2.6 0.0 copy-start.1
  2.6 1.0 %copy-done.1 = bf16[1024,256]{1,0:T(8,128)(2,1)S(1)} copy-done((bf16[1024,256]{1,0:T(8,128)(2,1)S(1)}, bf16[1024,256]{1,0:T(8,128)(2,1)}, u32[]{:S(2)}) %copy-start.1) | copy-done | bytes 524312
  3.6 0.0 copy-start.2
  3.6 0.9 %copy-done.2 = bf16[2,256,256]{2,1,0:T(8,128)(2,1)S(1)} copy-done((bf16[2,256,256]{2,1,0:T(8,128)(2,1)S(1)}, bf16[2,256,256]{2,1,0:T(8,128)(2,1)}, u32[]{:S(2)}) %copy-start.2) | copy-done | bytes 262168
  4.6 55.3 %shard_map.82 = bf16[1024,256]{1,0:T(8,128)(2,1)S(1)} custom-call(f32[2,8]{1,0:T(2,128)S(1)} %broadcast_multiply_fusion.fac_ref, bf16[1024,256]{1,0:T(8,128)(2,1)S(1)} %copy-done.1, s32[2,1024]{1,0:T(2,128)S(1)} %add_add_fusion.marks_ref, s32[1,1024]{1,0:T(1,128)S(1)} %bitcast.3, bf16[2,256,768]{2,1,0:T(8,128)(2,1)S(1)} %copy-done, ...), custom_call_target="tpu_custom_call" | custom-call | tf_op jit(solution)/shard_map/pallas_call | solution.py:273
  59.8 0.8 %copy.10 = bf16[1024,256]{1,0:T(8,128)(2,1)} copy(bf16[1024,256]{1,0:T(8,128)(2,1)S(1)} %shard_map.82) | data formatting | bytes 1048576
  (1 shorter events, 0.0 us)
Async XLA Ops:
  0.0 0.7 %copy-start.5 = (s32[1024]{0:T(1024)S(1)}, s32[1024]{0:T(1024)}, u32[]{:S(2)}) copy-start(s32[1024]{0:T(1024)} %param.10) | copy-start | bytes 12292
  0.0 0.7 %copy-start.6 = (f32[2,8]{1,0:T(2,128)S(1)}, f32[2,8]{1,0:T(2,128)}, u32[]{:S(2)}) copy-start(f32[2,8]{1,0:T(2,128)} %param.15) | copy-start | bytes 196
  0.7 0.7 %copy-start.3 = (s32[1024]{0:T(1024)S(1)}, s32[1024]{0:T(1024)}, u32[]{:S(2)}) copy-start(s32[1024]{0:T(1024)} %param.11) | copy-start | bytes 12292
  0.7 0.7 %copy-start.4 = (f32[2,256]{1,0:T(2,128)S(1)}, f32[2,256]{1,0:T(2,128)}, u32[]{:S(2)}) copy-start(f32[2,256]{1,0:T(2,128)} %gain_ref.1) | copy-start | bytes 6148
  1.5 1.1 %copy-start = (bf16[2,256,768]{2,1,0:T(8,128)(2,1)S(1)}, bf16[2,256,768]{2,1,0:T(8,128)(2,1)}, u32[]{:S(2)}) copy-start(bf16[2,256,768]{2,1,0:T(8,128)(2,1)} %w_ref.1) | copy-start | bytes 2359300
  2.6 1.0 %copy-start.1 = (bf16[1024,256]{1,0:T(8,128)(2,1)S(1)}, bf16[1024,256]{1,0:T(8,128)(2,1)}, u32[]{:S(2)}) copy-start(bf16[1024,256]{1,0:T(8,128)(2,1)} %h_ref.1) | copy-start | bytes 1572868
  3.6 0.9 %copy-start.2 = (bf16[2,256,256]{2,1,0:T(8,128)(2,1)S(1)}, bf16[2,256,256]{2,1,0:T(8,128)(2,1)}, u32[]{:S(2)}) copy-start(bf16[2,256,256]{2,1,0:T(8,128)(2,1)} %wo_ref.1) | copy-start | bytes 786436
